TPU v7x, 32 devices: a whole 2x2x4 slice. The times are simulated.
32 devices in a mesh: groups: 2 (over x), blk: 4 (over y, core), rows: 4 (over z).
Axes of the slice: x: 2, y: 2, z: 4, core: 2. Of those that a mesh axis runs over, the one named last changes fastest.
Arguments:
- frame_one: float32 [4096, 256], P(('groups', 'blk', 'rows')), parts along dimension 0, may hold values from -6 to 6
- frame_two: float32 [4096, 256], P(('groups', 'blk', 'rows')), parts along dimension 0, may hold values from -6 to 6
- cot_zero: float32 [4096, 2048], P(('groups', 'blk', 'rows')), parts along dimension 0, may hold values from -0.375 to 0.375
- cot_one: float32 [4096, 512], P(('groups', 'blk', 'rows')), parts along dimension 0, may hold values from -1.5 to 1.5
- cot_two: float32 [4096, 128], P(('groups', 'blk', 'rows')), parts along dimension 0, may hold values from -6 to 6
- cot_three: float32 [4096, 32], P(('groups', 'blk', 'rows')), parts along dimension 0, may hold values from -24 to 24
Outputs:
- corr_zero: float32 [4096, 2048], P(('groups', 'blk', 'rows')), parts along dimension 0
- corr_one: float32 [4096, 512], P(('groups', 'blk', 'rows')), parts along dimension 0
- corr_two: float32 [4096, 128], P(('groups', 'blk', 'rows')), parts along dimension 0
- corr_three: float32 [4096, 32], P(('groups', 'blk', 'rows')), parts along dimension 0
- grad_one: float32 [256, 4096], P('rows', ('groups', 'blk')), parts along dimension 1
- grad_two: float32 [256, 4096], P('rows', ('groups', 'blk')), parts along dimension 1
There are 2 independent parts, one for each index of `groups`. A program takes and returns all parts, laid end to end along the dimension named above; each array names one. Nothing has to cross between parts.
All inputs are finite; a program needn't handle non-finite values.
Results may differ from a plain program's by a relative error of at most 0.0001.
Values sent between devices are 32-bit elements; how exact they have to be, the bound alone decides.
A program may use at most 64 MiB of HBM per device.

v0:
```python
import math

import jax
import jax.numpy as jnp
from jax import lax
from jax.sharding import PartitionSpec as P

C = 256
LEVELS = 4
TROWS = 8
W2 = 64


highest = lax.Precision.HIGHEST


def shifted(value, axis, steps):
    count = lax.axis_size(axis)
    pairs = [(source, (source + steps) % count) for source in range(count)]
    return lax.ppermute(value, axis, pairs)


def pool_table(tile_rows, columns, levels):
    tile_size = tile_rows * columns
    pixels = jnp.arange(tile_size, dtype=jnp.int32)
    row_of = pixels // columns
    col_of = pixels % columns
    blocks = []
    for level_idx in range(1, levels):
        pooled_cols = columns >> level_idx
        pooled_size = tile_size >> 2 * level_idx
        target = (row_of >> level_idx) * pooled_cols + (col_of >> level_idx)
        member = target[:, None] == jnp.arange(pooled_size, dtype=jnp.int32)[None, :]
        blocks.append(member.astype(jnp.float32) * 0.25**level_idx)
    return jnp.concatenate(blocks, axis=1)


def move_forward(pieces):
    return (shifted(pieces[0], "blk", 1),)


def move_backward(pieces, accums):
    moved_piece, moved_acc = shifted((pieces[0], accums[0]), "blk", 1)
    return ((moved_piece,), (moved_acc,))


def move_home(accums):
    return (shifted(accums[0], "blk", 1),)


def on_device(frame_one, frame_two, cot_zero, cot_one, cot_two, cot_three):
    band_size = frame_one.shape[0]
    inv_root = 1.0 / math.sqrt(C)
    cycle_size = lax.axis_size("blk")
    position = lax.axis_index("blk")
    tile_f2 = lax.all_gather(frame_two, "rows", axis=0, tiled=True)
    tile_size = tile_f2.shape[0]
    table = pool_table(TROWS, W2, LEVELS)
    cots = (cot_zero, cot_one, cot_two, cot_three)
    widths = [tile_size >> 2 * level_idx for level_idx in range(LEVELS)]
    row_parts = (frame_one,)
    start_pieces = (tile_f2,)
    directions = (1,)

    def add_tile(volumes, rows_part, f2_piece, source):
        base = (
            lax.dot_general(
                rows_part,
                f2_piece,
                (((1,), (1,)), ((), ())),
                precision=highest,
                preferred_element_type=jnp.float32,
            )
            * inv_root
        )
        pooled = jnp.dot(base, table, precision=highest, preferred_element_type=jnp.float32)
        slab_parts = [base]
        offset = 0
        for level_idx in range(1, LEVELS):
            slab_parts.append(pooled[:, offset : offset + widths[level_idx]])
            offset = offset + widths[level_idx]
        updated = []
        for volume, slab_part in zip(volumes, slab_parts):
            start_col = source * slab_part.shape[1]
            current = lax.dynamic_slice_in_dim(volume, start_col, slab_part.shape[1], 1)
            updated.append(
                lax.dynamic_update_slice_in_dim(volume, current + slab_part, start_col, 1)
            )
        return tuple(updated)

    def tile_grad(source):
        slices = [
            lax.dynamic_slice_in_dim(cot, source * widths[level_idx], widths[level_idx], 1)
            for level_idx, cot in enumerate(cots)
        ]
        coarse = jnp.concatenate(slices[1:], axis=1)
        spread = lax.dot_general(
            coarse,
            table,
            (((1,), (1,)), ((), ())),
            precision=highest,
            preferred_element_type=jnp.float32,
        )
        return (slices[0] + spread) * inv_root

    def forward_work(volumes, pieces, step_idx):
        for rows_part, f2_piece, direction in zip(row_parts, pieces, directions):
            source = (position - direction * step_idx) % cycle_size
            volumes = add_tile(volumes, rows_part, f2_piece, source)
        return volumes

    def backward_work(grads, accums, pieces, step_idx):
        new_grads = []
        new_accums = []
        for rows_part, f2_piece, direction, grad_part, acc_part in zip(
            row_parts, pieces, directions, grads, accums
        ):
            source = (position - direction * step_idx) % cycle_size
            upstream = tile_grad(source)
            new_grads.append(
                grad_part
                + lax.dot_general(
                    f2_piece,
                    upstream,
                    (((0,), (1,)), ((), ())),
                    precision=highest,
                    preferred_element_type=jnp.float32,
                )
            )
            new_accums.append(
                acc_part
                + lax.dot_general(
                    rows_part,
                    upstream,
                    (((0,), (0,)), ((), ())),
                    precision=highest,
                    preferred_element_type=jnp.float32,
                )
            )
        return (tuple(new_grads), tuple(new_accums))

    volumes = tuple((jnp.zeros((band_size, cot.shape[1]), jnp.float32) for cot in cots))
    grads = tuple(
        (jnp.zeros((part_rows.shape[1], band_size), jnp.float32) for part_rows in row_parts)
    )
    accums = tuple(
        (jnp.zeros((part_rows.shape[1], tile_size), jnp.float32) for part_rows in row_parts)
    )
    last_step = cycle_size - 1

    def forward_step(step_idx, carry):
        volumes_now, pieces_now = carry
        volumes_now = forward_work(volumes_now, pieces_now, step_idx)
        return (volumes_now, move_forward(pieces_now))

    volumes, pieces = lax.fori_loop(0, last_step, forward_step, (volumes, start_pieces))
    volumes = forward_work(volumes, pieces, last_step)

    def backward_step(step_idx, carry):
        grads_now, accums_now, pieces_now = carry
        grads_now, accums_now = backward_work(grads_now, accums_now, pieces_now, step_idx)
        pieces_now, accums_now = move_backward(pieces_now, accums_now)
        return (grads_now, accums_now, pieces_now)

    grads, accums, pieces = lax.fori_loop(
        0, last_step, backward_step, (grads, accums, start_pieces)
    )
    grads, accums = backward_work(grads, accums, pieces, last_step)
    accums = move_home(accums)
    grad_stack = grads[0]
    acc_stack = accums[0]
    grad_two = lax.psum_scatter(acc_stack, "rows", scatter_dimension=0, tiled=True)
    grad_one = lax.all_to_all(grad_stack, "rows", split_axis=0, concat_axis=1, tiled=True)
    return (volumes[0], volumes[1], volumes[2], volumes[3], grad_one, grad_two)


def solution(mesh):
    return jax.shard_map(
        on_device,
        mesh=mesh,
        in_specs=(
            P(("groups", "blk", "rows"), None),
            P(("groups", "blk", "rows"), None),
            P(("groups", "blk", "rows"), None),
            P(("groups", "blk", "rows"), None),
            P(("groups", "blk", "rows"), None),
            P(("groups", "blk", "rows"), None),
        ),
        out_specs=(
            P(("groups", "blk", "rows"), None),
            P(("groups", "blk", "rows"), None),
            P(("groups", "blk", "rows"), None),
            P(("groups", "blk", "rows"), None),
            P("rows", ("groups", "blk")),
            P("rows", ("groups", "blk")),
        ),
        check_vma=False,
    )
```

profile of v0, /device:TPU:0, one launch (start us, length us, event | category | flops | bytes accessed | tf_op | source)
XLA Modules:
  0.0 160.6 jit_solution(15924149462514822327)
XLA Ops:
  7.3 0.7 copy-done.12
  8.4 0.8 copy-done.9
  9.2 17.3 %all_gather.3 = f32[512,256]{1,0:T(8,128)S(1)} all-gather(f32[128,256]{1,0:T(8,128)S(1)} %copy-done.9), channel_id=1, replica_groups=mesh['groups'=2,'blk'=4,'rows'=4] {'rows'}, dimensions={0}, use_global_device_ids=true | all-gather | bytes 655360 | tf_op jit(solution)/shard_map/all_gather | solution.py:56
  26.5 0.8 copy-done
  27.7 0.6 constant_dynamic-slice_fusion.4
  28.5 0.7 constant_dynamic-slice_fusion.3
  29.4 0.7 copy-done.3
  30.4 50.3 %while.44 = (s32[]{:T(128)}, f32[256,128]{0,1:T(8,128)S(1)}, f32[256,512]{0,1:T(8,128)S(1)}, f32[512,256]{1,0:T(8,128)S(1)}, s32[]{:T(128)}, /*index=5*/f32[128,...) while((s32[]{:T(128)}, f32[256,128]{0,1:T(8,128)S(1)}, ...), condition=%wide.region_3.4_spmd.clone, body=%wide.region_2.3_spmd.clone.sunk | while | flops 535144480 | bytes 8868432 | solution.py:165
  30.6 1.6 %fusion.92 = f32[128,512]{1,0:T(8,128)S(1)} fusion(f32[512,168]{1,0:T(8,128)S(1)} %get-tuple-element.851, f32[128,2048]{1,0:T(8,128)} %get-tuple-element.847, s32[]{:T(128)S(6)} %select_n.240, f32[128,8]{1,0:T(8,128)S(1)} %copy.40, f32[128,32]{1,0:T(8,128)S(1)} %constant_dynamic-slice_fusion.10, f32[128,128]{1,0:T(8,128)S(1)} %constant_dynamic-slice_fusion.11), kind=kOutput, calls=%fused_computation.11.clone.1 | convolution fusion | flops 132294656 | bytes 954372 | tf_op jit(solution)/shard_map/while/body/eval_jaxpr/dot_general | solution.py:97
  32.3 0.6 fusion.94
  33.0 1.7 %collective-permute-start.2 = (f32[512,256]{1,0:T(8,128)S(1)}, f32[512,256]{1,0:T(8,128)S(1)}, u32[]{:S(2)}, u32[]{:S(2)}) collective-permute-start(f32[512,256]{1,0:T(8,128)S(1)} %copy.74), channel_id=1, source_target_pairs={{0,4},{4,8},{8,12},{12,0},{1,5},{5,9},{9,13},{13,1},{2,6},{6,10},{... | collective-permute-start | bytes 1572872 | tf_op jit(solution)/shard_map/while/body/eval_jaxpr/ppermute | solution.py:20
  35.1 6.4 %collective-permute-done.1 = f32[256,512]{0,1:T(8,128)S(1)} collective-permute-done((f32[256,512]{0,1:T(8,128)S(1)}, f32[256,512]{0,1:T(8,128)S(1)}, u32[]{:S(2)}, u32[]{:S(2)}) %collective-permute-start.1) | collective-permute-done | bytes 524320 | tf_op jit(solution)/shard_map/while/body/eval_jaxpr/ppermute | solution.py:20
  41.6 5.6 %collective-permute-done.2 = f32[512,256]{1,0:T(8,128)S(1)} collective-permute-done((f32[512,256]{1,0:T(8,128)S(1)}, f32[512,256]{1,0:T(8,128)S(1)}, u32[]{:S(2)}, u32[]{:S(2)}) %collective-permute-start.2) | collective-permute-done | bytes 524320 | tf_op jit(solution)/shard_map/while/body/eval_jaxpr/ppermute | solution.py:20
  47.4 1.6 %fusion.92 = f32[128,512]{1,0:T(8,128)S(1)} fusion(f32[512,168]{1,0:T(8,128)S(1)} %get-tuple-element.851, f32[128,2048]{1,0:T(8,128)} %get-tuple-element.847, s32[]{:T(128)S(6)} %select_n.240, f32[128,8]{1,0:T(8,128)S(1)} %copy.40, f32[128,32]{1,0:T(8,128)S(1)} %constant_dynamic-slice_fusion.10, f32[128,128]{1,0:T(8,128)S(1)} %constant_dynamic-slice_fusion.11), kind=kOutput, calls=%fused_computation.11.clone.1 | convolution fusion | flops 132294656 | bytes 954372 | tf_op jit(solution)/shard_map/while/body/eval_jaxpr/dot_general | solution.py:97
  49.0 0.6 fusion.94
  49.8 1.7 %collective-permute-start.2 = (f32[512,256]{1,0:T(8,128)S(1)}, f32[512,256]{1,0:T(8,128)S(1)}, u32[]{:S(2)}, u32[]{:S(2)}) collective-permute-start(f32[512,256]{1,0:T(8,128)S(1)} %copy.74), channel_id=1, source_target_pairs={{0,4},{4,8},{8,12},{12,0},{1,5},{5,9},{9,13},{13,1},{2,6},{6,10},{... | collective-permute-start | bytes 1572872 | tf_op jit(solution)/shard_map/while/body/eval_jaxpr/ppermute | solution.py:20
  51.9 6.4 %collective-permute-done.1 = f32[256,512]{0,1:T(8,128)S(1)} collective-permute-done((f32[256,512]{0,1:T(8,128)S(1)}, f32[256,512]{0,1:T(8,128)S(1)}, u32[]{:S(2)}, u32[]{:S(2)}) %collective-permute-start.1) | collective-permute-done | bytes 524320 | tf_op jit(solution)/shard_map/while/body/eval_jaxpr/ppermute | solution.py:20
  58.3 5.6 %collective-permute-done.2 = f32[512,256]{1,0:T(8,128)S(1)} collective-permute-done((f32[512,256]{1,0:T(8,128)S(1)}, f32[512,256]{1,0:T(8,128)S(1)}, u32[]{:S(2)}, u32[]{:S(2)}) %collective-permute-start.2) | collective-permute-done | bytes 524320 | tf_op jit(solution)/shard_map/while/body/eval_jaxpr/ppermute | solution.py:20
  64.1 1.6 %fusion.92 = f32[128,512]{1,0:T(8,128)S(1)} fusion(f32[512,168]{1,0:T(8,128)S(1)} %get-tuple-element.851, f32[128,2048]{1,0:T(8,128)} %get-tuple-element.847, s32[]{:T(128)S(6)} %select_n.240, f32[128,8]{1,0:T(8,128)S(1)} %copy.40, f32[128,32]{1,0:T(8,128)S(1)} %constant_dynamic-slice_fusion.10, f32[128,128]{1,0:T(8,128)S(1)} %constant_dynamic-slice_fusion.11), kind=kOutput, calls=%fused_computation.11.clone.1 | convolution fusion | flops 132294656 | bytes 954372 | tf_op jit(solution)/shard_map/while/body/eval_jaxpr/dot_general | solution.py:97
  65.8 0.6 fusion.94
  66.5 1.7 %collective-permute-start.2 = (f32[512,256]{1,0:T(8,128)S(1)}, f32[512,256]{1,0:T(8,128)S(1)}, u32[]{:S(2)}, u32[]{:S(2)}) collective-permute-start(f32[512,256]{1,0:T(8,128)S(1)} %copy.74), channel_id=1, source_target_pairs={{0,4},{4,8},{8,12},{12,0},{1,5},{5,9},{9,13},{13,1},{2,6},{6,10},{... | collective-permute-start | bytes 1572872 | tf_op jit(solution)/shard_map/while/body/eval_jaxpr/ppermute | solution.py:20
  68.6 6.4 %collective-permute-done.1 = f32[256,512]{0,1:T(8,128)S(1)} collective-permute-done((f32[256,512]{0,1:T(8,128)S(1)}, f32[256,512]{0,1:T(8,128)S(1)}, u32[]{:S(2)}, u32[]{:S(2)}) %collective-permute-start.1) | collective-permute-done | bytes 524320 | tf_op jit(solution)/shard_map/while/body/eval_jaxpr/ppermute | solution.py:20
  75.1 5.6 %collective-permute-done.2 = f32[512,256]{1,0:T(8,128)S(1)} collective-permute-done((f32[512,256]{1,0:T(8,128)S(1)}, f32[512,256]{1,0:T(8,128)S(1)}, u32[]{:S(2)}, u32[]{:S(2)}) %collective-permute-start.2) | collective-permute-done | bytes 524320 | tf_op jit(solution)/shard_map/while/body/eval_jaxpr/ppermute | solution.py:20
  80.8 0.7 copy-done.7
  81.5 1.6 %fusion.13 = f32[128,512]{1,0:T(8,128)S(1)} fusion(f32[512,168]{1,0:T(8,128)S(1)} %get-tuple-element.863, f32[128,2048]{1,0:T(8,128)} %get-tuple-element.873, s32[]{:T(128)S(6)} %select_n.189, f32[128,8]{1,0:T(8,128)S(1)} %copy.30, f32[128,32]{1,0:T(8,128)S(1)} %copy-done.8, f32[128,128]{1,0:T(8,128)S(1)} %copy-done.7), kind=kOutput, calls=%fused_computation.27 | convolution fusion | flops 132294656 | bytes 954372 | tf_op jit(solution)/shard_map/dot_general | solution.py:97
  83.2 1.7 %convolution_add_fusion.2 = f32[256,128]{1,0:T(8,128)} fusion(f32[256,128]{1,0:T(8,128)S(1)} %copy.31, f32[512,256]{1,0:T(8,128)S(1)} %get-tuple-element.504, f32[128,512]{1,0:T(8,128)S(1)} %fusion.13), kind=kOutput, calls=%fused_computation.28 | convolution fusion | flops 201359360 | bytes 1048576 | tf_op jit(solution)/shard_map/dot_general | solution.py:122
  84.8 5.4 %all-to-all-start = ((f32[4,64,128]{2,1,0:T(8,128)}), f32[4,64,128]{2,1,0:T(8,128)}, u32[]{:S(2)}, u32[]{:S(2)}) async-start(f32[4,64,128]{2,1,0:T(8,128)} %bitcast.1), calls=%async_computation | async-start | bytes 262144 | tf_op jit(solution)/shard_map/all_to_all | solution.py:173
  90.2 1.4 fusion.12
  91.8 0.9 copy-done.1
  92.7 30.7 %while.43 = (s32[]{:T(128)}, f32[128,2048]{1,0:T(8,128)S(1)}, f32[128,512]{0,1:T(8,128)S(1)}, f32[128,128]{0,1:T(8,128)S(1)}, f32[128,32]{0,1:T(8,128)S(1)}, /*i...) while((s32[]{:T(128)}, f32[128,2048]{1,0:T(8,128)S(1)}, ...), condition=%wide.region_1.2_spmd, body=%wide.region_0.1_spmd.sunk | while | flops 333599744 | bytes 5538318 | solution.py:156
  92.8 1.7 %collective-permute-start = (f32[512,256]{1,0:T(8,128)S(1)}, f32[512,256]{1,0:T(8,128)S(1)}, u32[]{:S(2)}, u32[]{:S(2)}) collective-permute-start(f32[512,256]{1,0:T(8,128)S(1)} %copy.56), channel_id=1, source_target_pairs={{0,4},{4,8},{8,12},{12,0},{1,5},{5,9},{9,13},{13,1},{2,6},{6,10},{... | collective-permute-start | bytes 1572872 | tf_op jit(solution)/shard_map/while/body/eval_jaxpr/ppermute | solution.py:20
  94.4 0.6 add_dynamic-update-slice_fusion.2
  95.1 1.0 fusion.82
  96.1 9.9 %collective-permute-done = f32[512,256]{1,0:T(8,128)S(1)} collective-permute-done((f32[512,256]{1,0:T(8,128)S(1)}, f32[512,256]{1,0:T(8,128)S(1)}, u32[]{:S(2)}, u32[]{:S(2)}) %collective-permute-start) | collective-permute-done | bytes 524320 | tf_op jit(solution)/shard_map/while/body/eval_jaxpr/ppermute | solution.py:20
  106.2 0.6 add_dynamic-update-slice_fusion.2
  106.8 1.0 fusion.82
  107.9 6.9 %collective-permute-done = f32[512,256]{1,0:T(8,128)S(1)} collective-permute-done((f32[512,256]{1,0:T(8,128)S(1)}, f32[512,256]{1,0:T(8,128)S(1)}, u32[]{:S(2)}, u32[]{:S(2)}) %collective-permute-start) | collective-permute-done | bytes 524320 | tf_op jit(solution)/shard_map/while/body/eval_jaxpr/ppermute | solution.py:20
  114.9 0.6 add_dynamic-update-slice_fusion.2
  115.5 1.0 fusion.82
  116.6 6.9 %collective-permute-done = f32[512,256]{1,0:T(8,128)S(1)} collective-permute-done((f32[512,256]{1,0:T(8,128)S(1)}, f32[512,256]{1,0:T(8,128)S(1)}, u32[]{:S(2)}, u32[]{:S(2)}) %collective-permute-start) | collective-permute-done | bytes 524320 | tf_op jit(solution)/shard_map/while/body/eval_jaxpr/ppermute | solution.py:20
  123.6 0.8 copy.25
  124.4 1.3 copy.23
  125.7 1.5 bitcast_add_fusion
  127.4 1.0 fusion.41
  128.4 2.1 %copy.34 = f32[256,512]{1,0:T(8,128)} copy(f32[256,512]{0,1:T(8,128)} %collective-permute-done.3) | data formatting | bytes 1048576
  131.3 0.6 constant_dynamic-update-slice_fusion
  132.0 1.7 %copy_bitcast_fusion = f32[64,512]{1,0:T(8,128)} fusion(f32[4,64,128]{2,1,0:T(8,128)} %all-to-all-done), kind=kLoop, calls=%fused_computation.37 | loop fusion | bytes 262144 | tf_op jit(solution)/shard_map/all_to_all | solution.py:173
  133.7 20.0 %reduce-scatter.4.cloned.1.call-done = f32[64,512]{1,0:T(8,128)} async-done(((f32[256,512]{1,0:T(8,128)}), f32[64,512]{1,0:T(8,128)}) %reduce-scatter.4.cloned.1.call-update) | async-done | bytes 131088
  (84 shorter events, 5.4 us)
Async XLA Ops:
  7.2 0.7 copy-start.12
  8.3 0.9 copy-start.9
  26.5 0.8 copy-start
  26.5 1.1 copy-start.6
  27.7 0.8 copy-start.5
  29.2 0.9 copy-start.3
  29.4 1.1 copy-start.2
  32.9 8.7 %collective-permute-start.1 = (f32[256,512]{0,1:T(8,128)S(1)}, f32[256,512]{0,1:T(8,128)S(1)}, u32[]{:S(2)}, u32[]{:S(2)}) collective-permute-start(f32[256,512]{0,1:T(8,128)S(1)} %fusion.94), channel_id=1, source_target_pairs={{0,4},{4,8},{8,12},{12,0},{1,5},{5,9},{9,13},{13,1},{2,6},{6,10},{... | collective-permute-start | bytes 1572872 | tf_op jit(solution)/shard_map/while/body/eval_jaxpr/ppermute | solution.py:20
  33.0 14.2 %collective-permute-start.2 = (f32[512,256]{1,0:T(8,128)S(1)}, f32[512,256]{1,0:T(8,128)S(1)}, u32[]{:S(2)}, u32[]{:S(2)}) collective-permute-start(f32[512,256]{1,0:T(8,128)S(1)} %copy.74), channel_id=1, source_target_pairs={{0,4},{4,8},{8,12},{12,0},{1,5},{5,9},{9,13},{13,1},{2,6},{6,10},{... | collective-permute-start | bytes 1572872 | tf_op jit(solution)/shard_map/while/body/eval_jaxpr/ppermute | solution.py:20
  49.6 8.7 %collective-permute-start.1 = (f32[256,512]{0,1:T(8,128)S(1)}, f32[256,512]{0,1:T(8,128)S(1)}, u32[]{:S(2)}, u32[]{:S(2)}) collective-permute-start(f32[256,512]{0,1:T(8,128)S(1)} %fusion.94), channel_id=1, source_target_pairs={{0,4},{4,8},{8,12},{12,0},{1,5},{5,9},{9,13},{13,1},{2,6},{6,10},{... | collective-permute-start | bytes 1572872 | tf_op jit(solution)/shard_map/while/body/eval_jaxpr/ppermute | solution.py:20
  49.8 14.2 %collective-permute-start.2 = (f32[512,256]{1,0:T(8,128)S(1)}, f32[512,256]{1,0:T(8,128)S(1)}, u32[]{:S(2)}, u32[]{:S(2)}) collective-permute-start(f32[512,256]{1,0:T(8,128)S(1)} %copy.74), channel_id=1, source_target_pairs={{0,4},{4,8},{8,12},{12,0},{1,5},{5,9},{9,13},{13,1},{2,6},{6,10},{... | collective-permute-start | bytes 1572872 | tf_op jit(solution)/shard_map/while/body/eval_jaxpr/ppermute | solution.py:20
  66.4 8.7 %collective-permute-start.1 = (f32[256,512]{0,1:T(8,128)S(1)}, f32[256,512]{0,1:T(8,128)S(1)}, u32[]{:S(2)}, u32[]{:S(2)}) collective-permute-start(f32[256,512]{0,1:T(8,128)S(1)} %fusion.94), channel_id=1, source_target_pairs={{0,4},{4,8},{8,12},{12,0},{1,5},{5,9},{9,13},{13,1},{2,6},{6,10},{... | collective-permute-start | bytes 1572872 | tf_op jit(solution)/shard_map/while/body/eval_jaxpr/ppermute | solution.py:20
  66.5 14.2 %collective-permute-start.2 = (f32[512,256]{1,0:T(8,128)S(1)}, f32[512,256]{1,0:T(8,128)S(1)}, u32[]{:S(2)}, u32[]{:S(2)}) collective-permute-start(f32[512,256]{1,0:T(8,128)S(1)} %copy.74), channel_id=1, source_target_pairs={{0,4},{4,8},{8,12},{12,0},{1,5},{5,9},{9,13},{13,1},{2,6},{6,10},{... | collective-permute-start | bytes 1572872 | tf_op jit(solution)/shard_map/while/body/eval_jaxpr/ppermute | solution.py:20
  80.7 0.8 copy-start.7
  80.7 0.9 copy-start.8
  84.8 47.2 %all-to-all-start = ((f32[4,64,128]{2,1,0:T(8,128)}), f32[4,64,128]{2,1,0:T(8,128)}, u32[]{:S(2)}, u32[]{:S(2)}) async-start(f32[4,64,128]{2,1,0:T(8,128)} %bitcast.1), calls=%async_computation | async-start | bytes 262144 | tf_op jit(solution)/shard_map/all_to_all | solution.py:173
  90.2 63.5 %reduce-scatter.4.cloned.1.call-start = ((), (), s32[]{:S(2)}) async-start(), calls=%async_computation.2 | async-start | bytes 655360
  91.6 36.7 %collective-permute-start.3 = (f32[256,512]{0,1:T(8,128)}, f32[256,512]{0,1:T(8,128)}, u32[]{:S(2)}, u32[]{:S(2)}) collective-permute-start(f32[256,512]{0,1:T(8,128)} %fusion.12), channel_id=1, source_target_pairs={{0,4},{4,8},{8,12},{12,0},{1,5},{5,9},{9,13},{13,1},{2,6},{6,10},{... | collective-permute-start | bytes 1572872 | tf_op jit(solution)/shard_map/ppermute | solution.py:20
  91.7 1.0 copy-start.1
  92.8 13.3 %collective-permute-start = (f32[512,256]{1,0:T(8,128)S(1)}, f32[512,256]{1,0:T(8,128)S(1)}, u32[]{:S(2)}, u32[]{:S(2)}) collective-permute-start(f32[512,256]{1,0:T(8,128)S(1)} %copy.56), channel_id=1, source_target_pairs={{0,4},{4,8},{8,12},{12,0},{1,5},{5,9},{9,13},{13,1},{2,6},{6,10},{... | collective-permute-start | bytes 1572872 | tf_op jit(solution)/shard_map/while/body/eval_jaxpr/ppermute | solution.py:20
  106.1 8.7 %collective-permute-start = (f32[512,256]{1,0:T(8,128)S(1)}, f32[512,256]{1,0:T(8,128)S(1)}, u32[]{:S(2)}, u32[]{:S(2)}) collective-permute-start(f32[512,256]{1,0:T(8,128)S(1)} %copy.56), channel_id=1, source_target_pairs={{0,4},{4,8},{8,12},{12,0},{1,5},{5,9},{9,13},{13,1},{2,6},{6,10},{... | collective-permute-start | bytes 1572872 | tf_op jit(solution)/shard_map/while/body/eval_jaxpr/ppermute | solution.py:20
  114.8 8.7 %collective-permute-start = (f32[512,256]{1,0:T(8,128)S(1)}, f32[512,256]{1,0:T(8,128)S(1)}, u32[]{:S(2)}, u32[]{:S(2)}) collective-permute-start(f32[512,256]{1,0:T(8,128)S(1)} %copy.56), channel_id=1, source_target_pairs={{0,4},{4,8},{8,12},{12,0},{1,5},{5,9},{9,13},{13,1},{2,6},{6,10},{... | collective-permute-start | bytes 1572872 | tf_op jit(solution)/shard_map/while/body/eval_jaxpr/ppermute | solution.py:20
  131.3 0.7 copy-start.11
  132.0 21.7 %copy-start.4 = (f32[128,2048]{1,0:T(8,128)}, f32[128,2048]{1,0:T(8,128)S(1)}, u32[]{:S(2)}) copy-start(f32[128,2048]{1,0:T(8,128)S(1)} %constant_dynamic-update-slice_fusion.1) | copy-start | bytes 3145732
  132.0 1.7 %copy-start.10 = (f32[128,32]{0,1:T(8,128)}, f32[128,32]{0,1:T(8,128)S(1)}, u32[]{:S(2)}) copy-start(f32[128,32]{0,1:T(8,128)S(1)} %fusion.22) | copy-start | bytes 49156
Sparse Core Ops, SparseCore 0:
  130.6 23.0 reduce-scatter.3
where the time goes:
time: 161 us
  waiting for transfers between devices  79.8 us (50%)
  matrix products  20.1 us (12%)
  blocking collectives  17.3 us (11%)
  local copies, waits for them, and re-layouts  15.6 us (10%)
  between operations  14.3 us (9%)
  starting transfers between devices  12.4 us (8%)
    ppermute x10, waiting for transfers between devices, shifted(): return lax.ppermute(value, axis, pairs)  59.8 us
    unnamed x2, waiting for transfers between devices  20 us
    all_gather x1, blocking collectives, on_device(): tile_f2 = lax.all_gather(frame_two, 'rows', axis=0, tiled=True)  17.3 us
    unnamed x27, local copies, waits for them, and re-layouts  7.52 us
    ppermute x10, starting transfers between devices, shifted(): return lax.ppermute(value, axis, pairs)  6.98 us
    dot_general x4, matrix products, tile_grad(): lax.dot_general(coarse, table, (((1,), (1,)), ((), ())), precision=highes...  6.48 us
    all_to_all x1, starting transfers between devices, on_device(): lax.all_to_all(grad_stack, 'rows', split_axis=0, concat_axis=1, tiled=True)  5.38 us
    dot_general x4, matrix products, add_tile(): jnp.dot(base, table, precision=highest, preferred_element_type=jnp.float32)  3.95 us
  transfers between devices with their start and end apart: 12, of which 10 were waited for; matrix products, arithmetic and copies ran while one was open for 11% of the time, Pallas kernels for 0%

commit v1 on v0

v1 whole, which is shorter than its diff:
```python
import functools
import math

import jax
import jax.numpy as jnp
from jax import lax
from jax.experimental import pallas as pl
from jax.experimental.pallas import tpu as pltpu
from jax.sharding import PartitionSpec as P

TROWS = 8
W2 = 64
CORES = 2
TILE = TROWS * W2
POOL1 = TILE // 4
POOL2 = TILE // 16
POOL3 = TILE // 64
POOLED = 2 * POOL1

f32 = jnp.float32
bf16 = jnp.bfloat16


def split(x):
    high = x.astype(bf16)
    low = (x - high.astype(f32)).astype(bf16)
    return high, low


def mm(a, b, ca, cb):
    return lax.dot_general(a, b, (((ca,), (cb,)), ((), ())), preferred_element_type=f32)


def pool_table():
    shape = (TILE, POOLED)
    pixel = lax.broadcasted_iota(jnp.int32, shape, 0)
    slot = lax.broadcasted_iota(jnp.int32, shape, 1)
    row, col = pixel // W2, pixel % W2
    one = (row // 2) * (W2 // 2) + col // 2
    two = (row // 4) * (W2 // 4) + col // 4 + POOL1
    three = (row // 8) * (W2 // 8) + col // 8 + POOL1 + POOL2
    value = jnp.where(slot == one, 0.25, 0.0)
    value = jnp.where(slot == two, 0.0625, value)
    value = jnp.where(slot == three, 0.015625, value)
    return value.astype(bf16)


def kernel(tiles, rows_n, f1_in, f2_in, c0_in, c1_in, c2_in, c3_in,
           o0, o1, o2, o3, g1_out, g2_out,
           f1, f2, c0, c1, c2, c3, coarse, scaled, table, f1s, f1t, acc, cin, yin, zin,
           corr, pooled, b2, b3, gacc, g1t,
           in_sem, out_sem, ag_recv, zs_sem, ys_sem, cs_sem,
           rc_send, rc_recv, ry_send, ry_recv, rz_send, rz_recv, g_send, g_recv):
    band = f1.shape[0]
    chans = f1.shape[1]
    band2 = f2_in.shape[0]
    ys_n = tiles // CORES
    inv_root = 1.0 / math.sqrt(chans)
    blk = lax.axis_index("blk")
    z = lax.axis_index("rows")
    core = blk % CORES
    y = blk // CORES
    other = 1 - core
    sib = {"blk": y * CORES + other}

    def at_z(k):
        return (z + k) % rows_n

    def at_y(k):
        return (y + k) % ys_n

    def span(t, zz):
        return pl.ds(pl.multiple_of(t * TILE + zz * band2, 8), band2)

    loads = {}
    for i, (name, src, dst) in enumerate((
            ("f1", f1_in, f1), ("c3", c3_in, c3), ("c2", c2_in, c2), ("c1", c1_in, c1),
            ("c0", c0_in, c0), ("f2", f2_in, f2.at[span(blk, z), :]))):
        loads[name] = pltpu.make_async_copy(src, dst, in_sem.at[i])
        loads[name].start()

    peers = [{"rows": at_z(k)} for k in range(1, rows_n)]
    peers += [{"blk": at_y(k) * CORES + core} for k in range(1, ys_n)]
    peers += [sib]
    barrier = pltpu.get_barrier_semaphore()
    for peer in peers:
        pl.semaphore_signal(barrier, inc=1, device_id=peer)
    table[...] = pool_table()
    pl.semaphore_wait(barrier, len(peers))

    sent = []

    def send(src, dst, ssem, rsem, peer):
        copy = pltpu.make_async_remote_copy(
            src_ref=src, dst_ref=dst, send_sem=ssem, recv_sem=rsem,
            device_id=peer, device_id_type=pl.DeviceIdType.MESH)
        copy.start()
        sent.append(copy)

    def await_(ref, rsem):
        pltpu.make_async_copy(ref, ref, rsem).wait()

    def ag_wait(t, zz):
        await_(f2.at[span(t, zz), :], ag_recv.at[t * rows_n + zz])

    def to_sib(t, zz, src=None):
        where = f2.at[span(t, zz), :]
        i = t * rows_n + zz
        send(where if src is None else src, where, cs_sem.at[i], ag_recv.at[i], sib)

    def to_y(k, zz, src=None):
        where = f2.at[span(blk, zz), :]
        send(where if src is None else src, where, ys_sem.at[k - 1, zz],
             ag_recv.at[blk * rows_n + zz], {"blk": at_y(k) * CORES + core})

    order = sorted(range(1, rows_n), key=lambda k: -min(k, rows_n - k))
    own = f2.at[span(blk, z), :]
    for k in order:
        send(f2_in, own, zs_sem.at[k - 1], ag_recv.at[blk * rows_n + z], {"rows": at_z(k)})
    for k in range(1, ys_n):
        to_y(k, z, f2_in)
    to_sib(blk, z, f2_in)

    loads["f1"].wait()
    high, low = split(f1[...])
    f1s[0:band, :] = high
    f1s[band:, :] = low
    turned = f1[...].T
    high, low = split(turned)
    f1t[:, 0:band] = high
    f1t[:, band:] = low
    loads["c3"].wait()
    loads["c2"].wait()
    loads["c1"].wait()
    for t in range(tiles):
        coarse[t] = jnp.concatenate(
            [c1[:, t * POOL1:(t + 1) * POOL1], c2[:, t * POOL2:(t + 1) * POOL2],
             c3[:, t * POOL3:(t + 1) * POOL3],
             jnp.zeros((band, POOLED - POOL1 - POOL2 - POOL3), f32)], axis=1)
    loads["c0"].wait()

    def band_sum(t):
        high, low = split(coarse[t])
        spread = mm(jnp.concatenate([high, low], axis=0), table[...], 1, 1)
        total = c0[:, pl.ds(pl.multiple_of(t * TILE, TILE), TILE)] + (spread[:band] + spread[band:])
        high, low = split(total * inv_root)
        scaled[t, 0:band, :] = high
        scaled[t, band:, :] = low
        twice = jnp.concatenate([high, high], axis=0)
        value = mm(f1t[...], twice, 1, 0) + mm(f1t[:, 0:band], low, 1, 0)
        acc[t] = value.reshape(rows_n, chans // rows_n, TILE)

    for k in list(range(1, ys_n)) + [0]:
        yy = at_y(k)
        band_sum(yy * CORES + other)
        send(acc.at[yy * CORES + other], cin.at[yy], rc_send.at[yy], rc_recv.at[yy], sib)
        band_sum(yy * CORES + core)

    def chip_sum(yy):
        await_(cin.at[yy], rc_recv.at[yy])
        t = yy * CORES + core
        acc[t] += cin[yy]

    for k in range(1, ys_n):
        yy = at_y(k)
        chip_sum(yy)
        for j in order + [0]:
            zz = at_z(j)
            send(acc.at[yy * CORES + core, zz], yin.at[k - 1, zz], ry_send.at[k - 1, zz],
                 ry_recv.at[k - 1, zz], {"blk": yy * CORES + core})

    for k in reversed(order):
        zz = at_z(k)
        ag_wait(blk, zz)
        for j in range(1, ys_n):
            to_y(j, zz)
        to_sib(blk, zz)
    chip_sum(y)
    loads["f2"].wait()

    outs = []

    def emit(src, dst, sem):
        copy = pltpu.make_async_copy(src, dst, sem)
        copy.start()
        outs.append(copy)

    def tile_work(i, t):
        block = f2[pl.ds(pl.multiple_of(t * TILE, TILE), TILE), :]
        high, low = split(block)
        both = mm(f1s[...], high, 1, 1)
        value = (both[:band] + both[band:] + mm(f1s[0:band, :], low, 1, 1)) * inv_root
        corr[t] = value
        emit(corr.at[t], o0.at[:, pl.ds(pl.multiple_of(t * TILE, TILE), TILE)], out_sem.at[0, i])
        vh, vl = split(value)
        both = mm(jnp.concatenate([vh, vl], axis=0), table[...], 1, 0)
        pooled[t] = both[:band] + both[band:]
        emit(pooled.at[t, :, 0:POOL1], o1.at[:, pl.ds(pl.multiple_of(t * POOL1, POOL1), POOL1)],
             out_sem.at[1, i])
        both = mm(scaled[t], high, 1, 0)
        grad = both[:band] + both[band:] + mm(scaled[t, 0:band, :], low, 1, 0)
        if i == 0:
            gacc[...] = grad
        else:
            gacc[...] += grad

    tile_work(0, blk)

    for j in order + [0]:
        zz = at_z(j)
        for k in range(1, ys_n):
            await_(yin.at[k - 1, zz], ry_recv.at[k - 1, zz])
            acc[blk, zz] += yin[k - 1, zz]
        if j:
            send(acc.at[blk, zz], zin.at[j - 1], rz_send.at[j - 1], rz_recv.at[j - 1], {"rows": zz})

    for zz in range(rows_n):
        ag_wait(y * CORES + other, zz)
    tile_work(1, y * CORES + other)

    done = 2
    for k in range(1, ys_n):
        t = at_y(k) * CORES + core
        for j in [0] + list(reversed(order)):
            zz = at_z(j)
            ag_wait(t, zz)
            to_sib(t, zz)
        tile_work(done, t)
        done += 1
    for k in range(1, ys_n):
        t = at_y(k) * CORES + other
        for zz in range(rows_n):
            ag_wait(t, zz)
        tile_work(done, t)
        done += 1

    g1t[...] = gacc[...].T.reshape(rows_n, chans // rows_n, band)
    mine = pl.ds(pl.multiple_of(z * band, band), band)
    for k in order:
        zz = at_z(k)
        send(g1t.at[zz], g1_out.at[:, mine], g_send.at[k - 1], g_recv.at[k - 1], {"rows": zz})
    g1_out[:, mine] = g1t[z]
    b2[...] = jnp.concatenate([pooled[t, :, POOL1:POOL1 + POOL2] for t in range(tiles)], axis=1)
    emit(b2, o2, out_sem.at[2, 0])
    b3[...] = jnp.concatenate(
        [pooled[t, :, POOL1 + POOL2:POOL1 + POOL2 + POOL3] for t in range(tiles)], axis=1)
    emit(b3, o3, out_sem.at[2, 1])
    total = acc[blk, z]
    for k in range(1, rows_n):
        await_(zin.at[k - 1], rz_recv.at[k - 1])
        total += zin[k - 1]
    g2_out[...] = total
    for k in range(1, rows_n):
        zz = (z + rows_n - k) % rows_n
        await_(g1_out.at[:, pl.ds(pl.multiple_of(zz * band, band), band)], g_recv.at[k - 1])
    for copy in outs:
        copy.wait()
    for copy in sent:
        copy.wait_send()


def on_device(tiles, rows_n, frame_one, frame_two, cot_zero, cot_one, cot_two, cot_three):
    band, chans = frame_one.shape
    ys_n = tiles // CORES
    part = chans // rows_n
    cots = (cot_zero, cot_one, cot_two, cot_three)
    hbm = pl.BlockSpec(memory_space=pl.ANY)
    vmem = pl.BlockSpec(memory_space=pltpu.VMEM)
    dma = pltpu.SemaphoreType.DMA
    return pl.pallas_call(
        functools.partial(kernel, tiles, rows_n),
        out_shape=tuple(jax.ShapeDtypeStruct(cot.shape, f32) for cot in cots) + (
            jax.ShapeDtypeStruct((part, band * rows_n), f32),
            jax.ShapeDtypeStruct((part, TILE), f32)),
        in_specs=[hbm] * 6,
        out_specs=(hbm,) * 4 + (vmem,) * 2,
        scratch_shapes=[
            pltpu.VMEM((band, chans), f32),
            pltpu.VMEM((tiles * TILE, chans), f32),
            pltpu.VMEM(cot_zero.shape, f32),
            pltpu.VMEM(cot_one.shape, f32),
            pltpu.VMEM(cot_two.shape, f32),
            pltpu.VMEM(cot_three.shape, f32),
            pltpu.VMEM((tiles, band, POOLED), f32),
            pltpu.VMEM((tiles, 2 * band, TILE), bf16),
            pltpu.VMEM((TILE, POOLED), bf16),
            pltpu.VMEM((2 * band, chans), bf16),
            pltpu.VMEM((chans, 2 * band), bf16),
            pltpu.VMEM((tiles, rows_n, part, TILE), f32),
            pltpu.VMEM((ys_n, rows_n, part, TILE), f32),
            pltpu.VMEM((ys_n - 1, rows_n, part, TILE), f32),
            pltpu.VMEM((rows_n - 1, part, TILE), f32),
            pltpu.VMEM((tiles, band, TILE), f32),
            pltpu.VMEM((tiles, band, POOLED), f32),
            pltpu.VMEM(cot_two.shape, f32),
            pltpu.VMEM(cot_three.shape, f32),
            pltpu.VMEM((band, chans), f32),
            pltpu.VMEM((rows_n, part, band), f32),
            dma((6,)),
            dma((3, max(tiles, 2))),
            dma((tiles * rows_n,)),
            dma((rows_n - 1,)),
            dma((ys_n - 1, rows_n)),
            dma((tiles * rows_n,)),
            dma((ys_n,)), dma((ys_n,)),
            dma((ys_n - 1, rows_n)), dma((ys_n - 1, rows_n)),
            dma((rows_n - 1,)), dma((rows_n - 1,)),
            dma((rows_n - 1,)), dma((rows_n - 1,)),
        ],
        compiler_params=pltpu.CompilerParams(
            collective_id=0, has_side_effects=True, vmem_limit_bytes=58 << 20),
    )(frame_one, frame_two, *cots)


def solution(mesh):
    band = P(("groups", "blk", "rows"), None)
    turned = P("rows", ("groups", "blk"))
    return jax.shard_map(
        functools.partial(on_device, mesh.shape["blk"], mesh.shape["rows"]),
        mesh=mesh,
        in_specs=(band,) * 6,
        out_specs=(band,) * 4 + (turned,) * 2,
        check_vma=False,
    )
```

time: 161 us -> 46.9 us (0.29)
  waiting for transfers between devices: 79.8 us -> 0 us
  Pallas kernels: 0 us -> 37.2 us
  matrix products: 20.1 us -> 0 us
  blocking collectives: 17.3 us -> 0 us
  between operations: 14.3 us -> 0.65 us
  starting transfers between devices: 12.4 us -> 0 us
  local copies, waits for them, and re-layouts: 15.6 us -> 8.7 us
    ppermute x10 -> x0, waiting for transfers between devices: 59.8 us -> none  [shifted(): return lax.ppermute(value, axis, pairs)]
    pallas_call x0 -> x1, Pallas kernels: none -> 37.2 us  [on_device(): pl.pallas_call(functools.partial(kernel, tiles, rows_n), out_shape=tuple(...]
    dot_general x20 -> x0, matrix products: 20.1 us -> none  [the longest x4 6.48 us: tile_grad(): lax.dot_general(coarse, table, (((1,), (1,)), ((), ())), precision=highes...]
    unnamed x2 -> x0, waiting for transfers between devices: 20 us -> none
    all_gather x1 -> x0, blocking collectives: 17.3 us -> none  [on_device(): tile_f2 = lax.all_gather(frame_two, 'rows', axis=0, tiled=True)]
    ppermute x10 -> x0, starting transfers between devices: 6.98 us -> none  [shifted(): return lax.ppermute(value, axis, pairs)]
    all_to_all x1 -> x0, starting transfers between devices: 5.38 us -> none  [on_device(): lax.all_to_all(grad_stack, 'rows', split_axis=0, concat_axis=1, tiled=True)]
    while x7 -> x0, local copies, waits for them, and re-layouts: 2.43 us -> none  [the longest x3 2.23 us: on_device(): lax.fori_loop(0, last_step, forward_step, (volumes, start_pieces))]
  transfers between devices with their start and end apart: 12 -> 0, of which waited for: 10 -> 0; matrix products, arithmetic and copies ran while one was open for 11% -> 0% of each run, Pallas kernels for 0% -> 0%
where the time goes in v1:
time: 46.9 us; the launch traced here: 46.6 us
  Pallas kernels  37.2 us (79%)
  local copies, waits for them, and re-layouts  8.7 us (19%)
  between operations  0.65 us (1%)
    pallas_call x1, Pallas kernels, on_device(): pl.pallas_call(functools.partial(kernel, tiles, rows_n), out_shape=tuple(...  37.2 us
    unnamed x14, local copies, waits for them, and re-layouts  7.18 us
    pallas_call x1, local copies, waits for them, and re-layouts, on_device(): pl.pallas_call(functools.partial(kernel, tiles, rows_n), out_shape=tuple(...  1.52 us

profile of v1, /device:TPU:0, one launch (start us, length us, event | category | flops | bytes accessed | tf_op | source)
XLA Modules:
  0.0 46.6 jit_solution(1327650043999807173)
XLA Ops:
  0.6 1.4 %copy.12.c3_in = f32[128,32]{1,0:T(8,128)} copy(f32[128,32]{0,1:T(8,128)} %param.11) | data formatting | bytes 32768 | tf_op args[5]
  2.1 37.2 %shard_map.109 = (f32[128,2048]{1,0:T(8,128)}, f32[128,512]{1,0:T(8,128)}, f32[128,128]{1,0:T(8,128)}, f32[128,32]{1,0:T(8,128)}, f32[64,512]{1,0:T(8,128)}, /*index=5*/f32[64,512]{1,0:T(8,128)}) custom-call(f32[128,256]{1,0:T(8,128)} %f1_in.1, f32[128,256]{1,0:T(8,128)} %f2_in.1, f32[128,2048]{1,0:T(8,128)} %c0_in.1, f32[128,512]{1,0:T(8,128)} %c1_in.1, ...), custom_call_target="tpu_custom_call" | custom-call | tf_op jit(solution)/shard_map/pallas_call | solution.py:270
  39.3 1.5 %copy.13 = f32[128,32]{0,1:T(8,128)} copy(f32[128,32]{1,0:T(8,128)} %get-tuple-element.9) | data formatting | bytes 32768 | tf_op jit(solution)/shard_map/pallas_call | solution.py:270
  40.8 0.0 copy-start
  40.8 2.3 %copy.19 = f32[128,2048]{1,0:T(8,128)} copy(f32[128,2048]{1,0:T(8,128)} %get-tuple-element.18) | data formatting | bytes 2097152
  43.2 0.0 copy-done
  43.2 0.0 copy-start.3
  43.2 0.7 %copy.20 = f32[128,512]{1,0:T(8,128)} copy(f32[128,512]{1,0:T(8,128)S(1)} %copy-done) | data formatting | bytes 524288
  43.9 0.2 copy-done.3
  44.0 0.0 copy-start.2
  44.1 0.6 %copy.21 = f32[128,128]{1,0:T(8,128)} copy(f32[128,128]{1,0:T(8,128)S(1)} %copy-done.3) | data formatting | bytes 131072
  44.7 0.3 copy-done.2
  45.0 0.0 copy-start.1
  45.0 0.7 %copy.22 = f32[64,512]{1,0:T(8,128)} copy(f32[64,512]{1,0:T(8,128)S(1)} %copy-done.2) | data formatting | bytes 262144
  45.6 0.3 copy-done.1
  45.9 0.7 %copy.23 = f32[64,512]{1,0:T(8,128)} copy(f32[64,512]{1,0:T(8,128)S(1)} %copy-done.1) | data formatting | bytes 262144
Async XLA Ops:
  40.8 2.3 %copy-start = (f32[128,512]{1,0:T(8,128)S(1)}, f32[128,512]{1,0:T(8,128)}, u32[]{:S(2)}) copy-start(f32[128,512]{1,0:T(8,128)} %get-tuple-element.19) | copy-start | bytes 786436
  43.2 0.9 %copy-start.3 = (f32[128,128]{1,0:T(8,128)S(1)}, f32[128,128]{1,0:T(8,128)}, u32[]{:S(2)}) copy-start(f32[128,128]{1,0:T(8,128)} %get-tuple-element.20) | copy-start | bytes 196612
  44.0 0.9 %copy-start.2 = (f32[64,512]{1,0:T(8,128)S(1)}, f32[64,512]{1,0:T(8,128)}, u32[]{:S(2)}) copy-start(f32[64,512]{1,0:T(8,128)} %get-tuple-element.22) | copy-start | bytes 393220
  45.0 1.0 %copy-start.1 = (f32[64,512]{1,0:T(8,128)S(1)}, f32[64,512]{1,0:T(8,128)}, u32[]{:S(2)}) copy-start(f32[64,512]{1,0:T(8,128)} %get-tuple-element.23) | copy-start | bytes 393220

commit v2 on v1

--- a/solution.py
+++ b/solution.py
@@ -47,9 +47,9 @@
 
 def kernel(tiles, rows_n, f1_in, f2_in, c0_in, c1_in, c2_in, c3_in,
            o0, o1, o2, o3, g1_out, g2_out,
-           f1, f2, c0, c1, c2, c3, coarse, scaled, table, f1s, f1t, acc, cin, yin, zin,
-           corr, pooled, b2, b3, gacc, g1t,
-           in_sem, out_sem, ag_recv, zs_sem, ys_sem, cs_sem,
+           f1, f2, c0, c1, c2, c3t, coarse, scaled, table, f1s, f1t, acc, cin, yin, zin,
+           pooled, gacc, g1t,
+           in_sem, ag_recv, zs_sem, ys_sem, cs_sem,
            rc_send, rc_recv, ry_send, ry_recv, rz_send, rz_recv, g_send, g_recv):
     band = f1.shape[0]
     chans = f1.shape[1]
@@ -74,7 +74,7 @@
 
     loads = {}
     for i, (name, src, dst) in enumerate((
-            ("f1", f1_in, f1), ("c3", c3_in, c3), ("c2", c2_in, c2), ("c1", c1_in, c1),
+            ("f1", f1_in, f1), ("c3", c3_in, c3t), ("c2", c2_in, c2), ("c1", c1_in, c1),
             ("c0", c0_in, c0), ("f2", f2_in, f2.at[span(blk, z), :]))):
         loads[name] = pltpu.make_async_copy(src, dst, in_sem.at[i])
         loads[name].start()
@@ -132,6 +132,7 @@
     loads["c3"].wait()
     loads["c2"].wait()
     loads["c1"].wait()
+    c3 = c3t[...].T
     for t in range(tiles):
         coarse[t] = jnp.concatenate(
             [c1[:, t * POOL1:(t + 1) * POOL1], c2[:, t * POOL2:(t + 1) * POOL2],
@@ -178,25 +179,17 @@
     chip_sum(y)
     loads["f2"].wait()
 
-    outs = []
-
-    def emit(src, dst, sem):
-        copy = pltpu.make_async_copy(src, dst, sem)
-        copy.start()
-        outs.append(copy)
-
     def tile_work(i, t):
         block = f2[pl.ds(pl.multiple_of(t * TILE, TILE), TILE), :]
         high, low = split(block)
         both = mm(f1s[...], high, 1, 1)
         value = (both[:band] + both[band:] + mm(f1s[0:band, :], low, 1, 1)) * inv_root
-        corr[t] = value
-        emit(corr.at[t], o0.at[:, pl.ds(pl.multiple_of(t * TILE, TILE), TILE)], out_sem.at[0, i])
+        o0[:, pl.ds(pl.multiple_of(t * TILE, TILE), TILE)] = value
         vh, vl = split(value)
         both = mm(jnp.concatenate([vh, vl], axis=0), table[...], 1, 0)
-        pooled[t] = both[:band] + both[band:]
-        emit(pooled.at[t, :, 0:POOL1], o1.at[:, pl.ds(pl.multiple_of(t * POOL1, POOL1), POOL1)],
-             out_sem.at[1, i])
+        both = both[:band] + both[band:]
+        pooled[t] = both[:, POOL1:]
+        o1[:, pl.ds(pl.multiple_of(t * POOL1, POOL1), POOL1)] = both[:, :POOL1]
         both = mm(scaled[t], high, 1, 0)
         grad = both[:band] + both[band:] + mm(scaled[t, 0:band, :], low, 1, 0)
         if i == 0:
@@ -240,11 +233,8 @@
         zz = at_z(k)
         send(g1t.at[zz], g1_out.at[:, mine], g_send.at[k - 1], g_recv.at[k - 1], {"rows": zz})
     g1_out[:, mine] = g1t[z]
-    b2[...] = jnp.concatenate([pooled[t, :, POOL1:POOL1 + POOL2] for t in range(tiles)], axis=1)
-    emit(b2, o2, out_sem.at[2, 0])
-    b3[...] = jnp.concatenate(
-        [pooled[t, :, POOL1 + POOL2:POOL1 + POOL2 + POOL3] for t in range(tiles)], axis=1)
-    emit(b3, o3, out_sem.at[2, 1])
+    o2[...] = jnp.concatenate([pooled[t, :, :POOL2] for t in range(tiles)], axis=1)
+    o3[...] = jnp.concatenate([pooled[t, :, POOL2:POOL2 + POOL3] for t in range(tiles)], axis=1).T
     total = acc[blk, z]
     for k in range(1, rows_n):
         await_(zin.at[k - 1], rz_recv.at[k - 1])
@@ -253,10 +243,17 @@
     for k in range(1, rows_n):
         zz = (z + rows_n - k) % rows_n
         await_(g1_out.at[:, pl.ds(pl.multiple_of(zz * band, band), band)], g_recv.at[k - 1])
-    for copy in outs:
-        copy.wait()
     for copy in sent:
         copy.wait_send()
+
+
+def store(*refs):
+    sems = refs[12]
+    copies = [pltpu.make_async_copy(refs[i], refs[6 + i], sems.at[i]) for i in range(6)]
+    for copy in copies:
+        copy.start()
+    for copy in copies:
+        copy.wait()
 
 
 def on_device(tiles, rows_n, frame_one, frame_two, cot_zero, cot_one, cot_two, cot_three):
@@ -267,20 +264,20 @@
     hbm = pl.BlockSpec(memory_space=pl.ANY)
     vmem = pl.BlockSpec(memory_space=pltpu.VMEM)
     dma = pltpu.SemaphoreType.DMA
-    return pl.pallas_call(
+    shapes = tuple(cot.shape for cot in cots[:3]) + (
+        cot_three.shape[::-1], (part, band * rows_n), (part, TILE))
+    made = pl.pallas_call(
         functools.partial(kernel, tiles, rows_n),
-        out_shape=tuple(jax.ShapeDtypeStruct(cot.shape, f32) for cot in cots) + (
-            jax.ShapeDtypeStruct((part, band * rows_n), f32),
-            jax.ShapeDtypeStruct((part, TILE), f32)),
-        in_specs=[hbm] * 6,
-        out_specs=(hbm,) * 4 + (vmem,) * 2,
+        out_shape=tuple(pltpu.VMEM(shape, f32) for shape in shapes),
+        in_specs=[pl.BlockSpec(memory_space=pltpu.HBM)] * 6,
+        out_specs=(vmem,) * 6,
         scratch_shapes=[
             pltpu.VMEM((band, chans), f32),
             pltpu.VMEM((tiles * TILE, chans), f32),
             pltpu.VMEM(cot_zero.shape, f32),
             pltpu.VMEM(cot_one.shape, f32),
             pltpu.VMEM(cot_two.shape, f32),
-            pltpu.VMEM(cot_three.shape, f32),
+            pltpu.VMEM(cot_three.shape[::-1], f32),
             pltpu.VMEM((tiles, band, POOLED), f32),
             pltpu.VMEM((tiles, 2 * band, TILE), bf16),
             pltpu.VMEM((TILE, POOLED), bf16),
@@ -290,14 +287,10 @@
             pltpu.VMEM((ys_n, rows_n, part, TILE), f32),
             pltpu.VMEM((ys_n - 1, rows_n, part, TILE), f32),
             pltpu.VMEM((rows_n - 1, part, TILE), f32),
-            pltpu.VMEM((tiles, band, TILE), f32),
-            pltpu.VMEM((tiles, band, POOLED), f32),
-            pltpu.VMEM(cot_two.shape, f32),
-            pltpu.VMEM(cot_three.shape, f32),
+            pltpu.VMEM((tiles, band, POOLED - POOL1), f32),
             pltpu.VMEM((band, chans), f32),
             pltpu.VMEM((rows_n, part, band), f32),
             dma((6,)),
-            dma((3, max(tiles, 2))),
             dma((tiles * rows_n,)),
             dma((rows_n - 1,)),
             dma((ys_n - 1, rows_n)),
@@ -308,8 +301,18 @@
             dma((rows_n - 1,)), dma((rows_n - 1,)),
         ],
         compiler_params=pltpu.CompilerParams(
-            collective_id=0, has_side_effects=True, vmem_limit_bytes=58 << 20),
-    )(frame_one, frame_two, *cots)
+            collective_id=0, has_side_effects=True, vmem_limit_bytes=48 << 20),
+    )(*[pltpu.with_memory_space_constraint(value, pltpu.HBM) for value in (
+        frame_one, frame_two, cot_zero, cot_one, cot_two, cot_three.T)])
+    placed = pl.pallas_call(
+        store,
+        out_shape=tuple(jax.ShapeDtypeStruct(shape, f32) for shape in shapes),
+        in_specs=[hbm] * 6,
+        out_specs=(hbm,) * 6,
+        scratch_shapes=[dma((6,))],
+        compiler_params=pltpu.CompilerParams(vmem_limit_bytes=1 << 20),
+    )(*[pltpu.with_memory_space_constraint(value, pltpu.VMEM) for value in made])
+    return placed[:3] + (placed[3].T,) + placed[4:]
 
 
 def solution(mesh):

time: 46.9 us -> 38.5 us (0.82)
  local copies, waits for them, and re-layouts: 8.7 us -> 0 us
  Pallas kernels: 37.2 us -> 37.7 us
    unnamed x14 -> x0, local copies, waits for them, and re-layouts: 7.18 us -> none
    pallas_call x1 -> x0, local copies, waits for them, and re-layouts: 1.52 us -> none  [on_device(): pl.pallas_call(functools.partial(kernel, tiles, rows_n), out_shape=tuple(...]
    pallas_call x0 -> x1, Pallas kernels: none -> 1.21 us  [on_device(): pl.pallas_call(store, out_shape=tuple((jax.ShapeDtypeStruct(shape, f32) f...]
    pallas_call x1, Pallas kernels: 37.2 us -> 36.5 us  [on_device(): pl.pallas_call(functools.partial(kernel, tiles, rows_n), out_shape=tuple(...]
where the time goes in v2:
time: 38.5 us; the launch traced here: 38.3 us
  Pallas kernels  37.7 us (98%)
  between operations  0.64 us (2%)
    pallas_call x1, Pallas kernels, on_device(): pl.pallas_call(functools.partial(kernel, tiles, rows_n), out_shape=tuple(...  36.5 us
    pallas_call x1, Pallas kernels, on_device(): pl.pallas_call(store, out_shape=tuple((jax.ShapeDtypeStruct(shape, f32) f...  1.21 us

profile of v2, /device:TPU:0, one launch (start us, length us, event | category | flops | bytes accessed | tf_op | source)
XLA Modules:
  0.0 38.3 jit_solution(6127890143990824828)
XLA Ops:
  0.6 36.5 %shard_map.109 = (f32[128,2048]{1,0:T(8,128)S(1)}, f32[128,512]{1,0:T(8,128)S(1)}, f32[128,128]{1,0:T(8,128)S(1)}, f32[32,128]{1,0:T(8,128)S(1)}, f32[64,512]{1,0:T(8,128)S(1)}, /*index=5*/f32[64,512]{1,0:T(8,128)S(1)}) custom-call(f32[128,256]{1,0:T(8,128)} %f1_in.1, f32[128,256]{1,0:T(8,128)} %f2_in.1, f32[128,2048]{1,0:T(8,128)} %c0_in.1, ...), custom_call_target="tpu_custom_call" | custom-call | tf_op jit(solution)/shard_map/pallas_call | solution.py:269
  37.1 1.2 %shard_map.110 = (f32[128,2048]{1,0:T(8,128)}, f32[128,512]{1,0:T(8,128)}, f32[128,128]{1,0:T(8,128)}, f32[32,128]{1,0:T(8,128)}, f32[64,512]{1,0:T(8,128)}, /*index=5*/f32[64,512]{1,0:T(8,128)}) custom-call(f32[128,2048]{1,0:T(8,128)S(1)} %get-tuple-element.18.refs_0_, f32[128,512]{1,0:T(8,128)S(1)} %get-tuple-element.19.refs_1_, ...), custom_call_target="tpu_custom_call" | custom-call | tf_op jit(solution)/shard_map/pallas_call | solution.py:307

commit v3 on v2

--- a/solution.py
+++ b/solution.py
@@ -33,12 +33,13 @@
 
 def pool_table():
     shape = (TILE, POOLED)
-    pixel = lax.broadcasted_iota(jnp.int32, shape, 0)
+    pixel = lax.broadcasted_iota(jnp.int32, (TILE, 1), 0)
+    row, col = pixel // W2, pixel % W2
+    one = lax.shift_right_logical(row, 1) * (W2 // 2) + lax.shift_right_logical(col, 1)
+    two = lax.shift_right_logical(row, 2) * (W2 // 4) + lax.shift_right_logical(col, 2) + POOL1
+    three = lax.shift_right_logical(row, 3) * (W2 // 8) + lax.shift_right_logical(col, 3) + (
+        POOL1 + POOL2)
     slot = lax.broadcasted_iota(jnp.int32, shape, 1)
-    row, col = pixel // W2, pixel % W2
-    one = (row // 2) * (W2 // 2) + col // 2
-    two = (row // 4) * (W2 // 4) + col // 4 + POOL1
-    three = (row // 8) * (W2 // 8) + col // 8 + POOL1 + POOL2
     value = jnp.where(slot == one, 0.25, 0.0)
     value = jnp.where(slot == two, 0.0625, value)
     value = jnp.where(slot == three, 0.015625, value)
@@ -85,7 +86,6 @@
     barrier = pltpu.get_barrier_semaphore()
     for peer in peers:
         pl.semaphore_signal(barrier, inc=1, device_id=peer)
-    table[...] = pool_table()
     pl.semaphore_wait(barrier, len(peers))
 
     sent = []
@@ -121,6 +121,7 @@
         to_y(k, z, f2_in)
     to_sib(blk, z, f2_in)
 
+    table[...] = pool_table()
     loads["f1"].wait()
     high, low = split(f1[...])
     f1s[0:band, :] = high
@@ -162,13 +163,19 @@
         t = yy * CORES + core
         acc[t] += cin[yy]
 
-    for k in range(1, ys_n):
+    pieces = order + [0]
+    early, late = pieces[:rows_n - 1], pieces[rows_n - 1:]
+
+    def sums_to_y(k, some):
         yy = at_y(k)
-        chip_sum(yy)
-        for j in order + [0]:
+        for j in some:
             zz = at_z(j)
             send(acc.at[yy * CORES + core, zz], yin.at[k - 1, zz], ry_send.at[k - 1, zz],
                  ry_recv.at[k - 1, zz], {"blk": yy * CORES + core})
+
+    for k in range(1, ys_n):
+        chip_sum(at_y(k))
+        sums_to_y(k, early)
 
     for k in reversed(order):
         zz = at_z(k)
@@ -176,6 +183,8 @@
         for j in range(1, ys_n):
             to_y(j, zz)
         to_sib(blk, zz)
+    for k in range(1, ys_n):
+        sums_to_y(k, late)
     chip_sum(y)
     loads["f2"].wait()
 
@@ -199,13 +208,17 @@
 
     tile_work(0, blk)
 
-    for j in order + [0]:
-        zz = at_z(j)
-        for k in range(1, ys_n):
-            await_(yin.at[k - 1, zz], ry_recv.at[k - 1, zz])
-            acc[blk, zz] += yin[k - 1, zz]
-        if j:
-            send(acc.at[blk, zz], zin.at[j - 1], rz_send.at[j - 1], rz_recv.at[j - 1], {"rows": zz})
+    def sums_to_rows(some):
+        for j in some:
+            zz = at_z(j)
+            for k in range(1, ys_n):
+                await_(yin.at[k - 1, zz], ry_recv.at[k - 1, zz])
+                acc[blk, zz] += yin[k - 1, zz]
+            if j:
+                send(acc.at[blk, zz], zin.at[j - 1], rz_send.at[j - 1], rz_recv.at[j - 1],
+                     {"rows": zz})
+
+    sums_to_rows(early)
 
     for zz in range(rows_n):
         ag_wait(y * CORES + other, zz)
@@ -233,6 +246,7 @@
         zz = at_z(k)
         send(g1t.at[zz], g1_out.at[:, mine], g_send.at[k - 1], g_recv.at[k - 1], {"rows": zz})
     g1_out[:, mine] = g1t[z]
+    sums_to_rows(late)
     o2[...] = jnp.concatenate([pooled[t, :, :POOL2] for t in range(tiles)], axis=1)
     o3[...] = jnp.concatenate([pooled[t, :, POOL2:POOL2 + POOL3] for t in range(tiles)], axis=1).T
     total = acc[blk, z]

time: 38.5 us -> 36.7 us (0.953)
  Pallas kernels: 37.7 us -> 35.9 us
    pallas_call x1, Pallas kernels: 36.5 us -> 34.7 us  [on_device(): pl.pallas_call(functools.partial(kernel, tiles, rows_n), out_shape=tuple(...]
where the time goes in v3:
time: 36.7 us; the launch traced here: 36.6 us
  Pallas kernels  35.9 us (98%)
  between operations  0.64 us (2%)
    pallas_call x1, Pallas kernels, on_device(): pl.pallas_call(functools.partial(kernel, tiles, rows_n), out_shape=tuple(...  34.7 us
    pallas_call x1, Pallas kernels, on_device(): pl.pallas_call(store, out_shape=tuple((jax.ShapeDtypeStruct(shape, f32) f...  1.21 us

profile of v3, /device:TPU:0, one launch (start us, length us, event | category | flops | bytes accessed | tf_op | source)
XLA Modules:
  0.0 36.6 jit_solution(12255570559090891934)
XLA Ops:
  0.6 34.7 %shard_map.109 = (f32[128,2048]{1,0:T(8,128)S(1)}, f32[128,512]{1,0:T(8,128)S(1)}, f32[128,128]{1,0:T(8,128)S(1)}, f32[32,128]{1,0:T(8,128)S(1)}, f32[64,512]{1,0:T(8,128)S(1)}, /*index=5*/f32[64,512]{1,0:T(8,128)S(1)}) custom-call(f32[128,256]{1,0:T(8,128)} %f1_in.1, f32[128,256]{1,0:T(8,128)} %f2_in.1, f32[128,2048]{1,0:T(8,128)} %c0_in.1, ...), custom_call_target="tpu_custom_call" | custom-call | tf_op jit(solution)/shard_map/pallas_call | solution.py:283
  35.4 1.2 %shard_map.110 = (f32[128,2048]{1,0:T(8,128)}, f32[128,512]{1,0:T(8,128)}, f32[128,128]{1,0:T(8,128)}, f32[32,128]{1,0:T(8,128)}, f32[64,512]{1,0:T(8,128)}, /*index=5*/f32[64,512]{1,0:T(8,128)}) custom-call(f32[128,2048]{1,0:T(8,128)S(1)} %get-tuple-element.18.refs_0_, f32[128,512]{1,0:T(8,128)S(1)} %get-tuple-element.19.refs_1_, ...), custom_call_target="tpu_custom_call" | custom-call | tf_op jit(solution)/shard_map/pallas_call | solution.py:321

commit v4 on v3

--- a/solution.py
+++ b/solution.py
@@ -51,7 +51,7 @@
            f1, f2, c0, c1, c2, c3t, coarse, scaled, table, f1s, f1t, acc, cin, yin, zin,
            pooled, gacc, g1t,
            in_sem, ag_recv, zs_sem, ys_sem, cs_sem,
-           rc_send, rc_recv, ry_send, ry_recv, rz_send, rz_recv, g_send, g_recv):
+           rc_send, rc_recv, ry_send, ry_recv, rz_send, rz_recv, g_send, g_recv, zf_sem):
     band = f1.shape[0]
     chans = f1.shape[1]
     band2 = f2_in.shape[0]
@@ -65,7 +65,12 @@
     sib = {"blk": y * CORES + other}
 
     def at_z(k):
-        return (z + k) % rows_n
+        zz, bit = z, 1
+        while bit < rows_n:
+            if k % (2 * bit) >= bit:
+                zz = zz + bit - 2 * bit * (z // bit % 2)
+            bit *= 2
+        return zz
 
     def at_y(k):
         return (y + k) % ys_n
@@ -86,41 +91,6 @@
     barrier = pltpu.get_barrier_semaphore()
     for peer in peers:
         pl.semaphore_signal(barrier, inc=1, device_id=peer)
-    pl.semaphore_wait(barrier, len(peers))
-
-    sent = []
-
-    def send(src, dst, ssem, rsem, peer):
-        copy = pltpu.make_async_remote_copy(
-            src_ref=src, dst_ref=dst, send_sem=ssem, recv_sem=rsem,
-            device_id=peer, device_id_type=pl.DeviceIdType.MESH)
-        copy.start()
-        sent.append(copy)
-
-    def await_(ref, rsem):
-        pltpu.make_async_copy(ref, ref, rsem).wait()
-
-    def ag_wait(t, zz):
-        await_(f2.at[span(t, zz), :], ag_recv.at[t * rows_n + zz])
-
-    def to_sib(t, zz, src=None):
-        where = f2.at[span(t, zz), :]
-        i = t * rows_n + zz
-        send(where if src is None else src, where, cs_sem.at[i], ag_recv.at[i], sib)
-
-    def to_y(k, zz, src=None):
-        where = f2.at[span(blk, zz), :]
-        send(where if src is None else src, where, ys_sem.at[k - 1, zz],
-             ag_recv.at[blk * rows_n + zz], {"blk": at_y(k) * CORES + core})
-
-    order = sorted(range(1, rows_n), key=lambda k: -min(k, rows_n - k))
-    own = f2.at[span(blk, z), :]
-    for k in order:
-        send(f2_in, own, zs_sem.at[k - 1], ag_recv.at[blk * rows_n + z], {"rows": at_z(k)})
-    for k in range(1, ys_n):
-        to_y(k, z, f2_in)
-    to_sib(blk, z, f2_in)
-
     table[...] = pool_table()
     loads["f1"].wait()
     high, low = split(f1[...])
@@ -139,6 +109,41 @@
             [c1[:, t * POOL1:(t + 1) * POOL1], c2[:, t * POOL2:(t + 1) * POOL2],
              c3[:, t * POOL3:(t + 1) * POOL3],
              jnp.zeros((band, POOLED - POOL1 - POOL2 - POOL3), f32)], axis=1)
+    pl.semaphore_wait(barrier, len(peers))
+
+    sent = []
+
+    def send(src, dst, ssem, rsem, peer):
+        copy = pltpu.make_async_remote_copy(
+            src_ref=src, dst_ref=dst, send_sem=ssem, recv_sem=rsem,
+            device_id=peer, device_id_type=pl.DeviceIdType.MESH)
+        copy.start()
+        sent.append(copy)
+
+    def await_(ref, rsem):
+        pltpu.make_async_copy(ref, ref, rsem).wait()
+
+    def ag_wait(t, zz):
+        await_(f2.at[span(t, zz), :], ag_recv.at[t * rows_n + zz])
+
+    def to_sib(t, zz, src=None):
+        where = f2.at[span(t, zz), :]
+        i = t * rows_n + zz
+        send(where if src is None else src, where, cs_sem.at[i], ag_recv.at[i], sib)
+
+    def to_y(k, zz, src=None):
+        where = f2.at[span(blk, zz), :]
+        send(where if src is None else src, where, ys_sem.at[k - 1, zz],
+             ag_recv.at[blk * rows_n + zz], {"blk": at_y(k) * CORES + core})
+
+    order = sorted(range(1, rows_n), key=lambda k: (k & -k, k), reverse=True)
+    own = f2.at[span(blk, z), :]
+    for k in reversed(order):
+        send(f2_in, own, zs_sem.at[k - 1], ag_recv.at[blk * rows_n + z], {"rows": at_z(k)})
+    for k in range(1, ys_n):
+        to_y(k, z, f2_in)
+    to_sib(blk, z, f2_in)
+
     loads["c0"].wait()
 
     def band_sum(t):
@@ -177,11 +182,19 @@
         chip_sum(at_y(k))
         sums_to_y(k, early)
 
+    for k in range(1, ys_n):
+        t = at_y(k) * CORES + core
+        ag_wait(t, z)
+        where = f2.at[span(t, z), :]
+        send(where, where, zf_sem.at[k - 1], ag_recv.at[t * rows_n + z], {"rows": at_z(1)})
+        to_sib(t, z)
+
     for k in reversed(order):
         zz = at_z(k)
         ag_wait(blk, zz)
-        for j in range(1, ys_n):
-            to_y(j, zz)
+        if k != 1:
+            for j in range(1, ys_n):
+                to_y(j, zz)
         to_sib(blk, zz)
     for k in range(1, ys_n):
         sums_to_y(k, late)
@@ -206,7 +219,6 @@
         else:
             gacc[...] += grad
 
-    tile_work(0, blk)
 
     def sums_to_rows(some):
         for j in some:
@@ -219,6 +231,7 @@
                      {"rows": zz})
 
     sums_to_rows(early)
+    tile_work(0, blk)
 
     for zz in range(rows_n):
         ag_wait(y * CORES + other, zz)
@@ -227,7 +240,7 @@
     done = 2
     for k in range(1, ys_n):
         t = at_y(k) * CORES + core
-        for j in [0] + list(reversed(order)):
+        for j in [1] + [k for k in reversed(order) if k != 1]:
             zz = at_z(j)
             ag_wait(t, zz)
             to_sib(t, zz)
@@ -255,7 +268,7 @@
         total += zin[k - 1]
     g2_out[...] = total
     for k in range(1, rows_n):
-        zz = (z + rows_n - k) % rows_n
+        zz = at_z(k)
         await_(g1_out.at[:, pl.ds(pl.multiple_of(zz * band, band), band)], g_recv.at[k - 1])
     for copy in sent:
         copy.wait_send()
@@ -313,6 +326,7 @@
             dma((ys_n - 1, rows_n)), dma((ys_n - 1, rows_n)),
             dma((rows_n - 1,)), dma((rows_n - 1,)),
             dma((rows_n - 1,)), dma((rows_n - 1,)),
+            dma((ys_n - 1,)),
         ],
         compiler_params=pltpu.CompilerParams(
             collective_id=0, has_side_effects=True, vmem_limit_bytes=48 << 20),

time: 36.7 us -> 33.9 us (0.924)
  Pallas kernels: 35.9 us -> 33.2 us
    pallas_call x1, Pallas kernels: 34.7 us -> 31.9 us  [on_device(): pl.pallas_call(functools.partial(kernel, tiles, rows_n), out_shape=tuple(...]
where the time goes in v4:
time: 33.9 us; the launch traced here: 33.8 us
  Pallas kernels  33.2 us (98%)
  between operations  0.64 us (2%)
    pallas_call x1, Pallas kernels, on_device(): pl.pallas_call(functools.partial(kernel, tiles, rows_n), out_shape=tuple(...  31.9 us
    pallas_call x1, Pallas kernels, on_device(): pl.pallas_call(store, out_shape=tuple((jax.ShapeDtypeStruct(shape, f32) f...  1.21 us

profile of v4, /device:TPU:0, one launch (start us, length us, event | category | flops | bytes accessed | tf_op | source)
XLA Modules:
  0.0 33.8 jit_solution(1573180924705342156)
XLA Ops:
  0.6 31.9 %shard_map.109 = (f32[128,2048]{1,0:T(8,128)S(1)}, f32[128,512]{1,0:T(8,128)S(1)}, f32[128,128]{1,0:T(8,128)S(1)}, f32[32,128]{1,0:T(8,128)S(1)}, f32[64,512]{1,0:T(8,128)S(1)}, /*index=5*/f32[64,512]{1,0:T(8,128)S(1)}) custom-call(f32[128,256]{1,0:T(8,128)} %f1_in.1, f32[128,256]{1,0:T(8,128)} %f2_in.1, f32[128,2048]{1,0:T(8,128)} %c0_in.1, ...), custom_call_target="tpu_custom_call" | custom-call | tf_op jit(solution)/shard_map/pallas_call | solution.py:296
  32.6 1.2 %shard_map.110 = (f32[128,2048]{1,0:T(8,128)}, f32[128,512]{1,0:T(8,128)}, f32[128,128]{1,0:T(8,128)}, f32[32,128]{1,0:T(8,128)}, f32[64,512]{1,0:T(8,128)}, /*index=5*/f32[64,512]{1,0:T(8,128)}) custom-call(f32[128,2048]{1,0:T(8,128)S(1)} %get-tuple-element.18.refs_0_, f32[128,512]{1,0:T(8,128)S(1)} %get-tuple-element.19.refs_1_, ...), custom_call_target="tpu_custom_call" | custom-call | tf_op jit(solution)/shard_map/pallas_call | solution.py:335
